TPU v7x, 32 devices: a whole 2x2x4 slice. The times are simulated.
32 devices in a mesh: dp: 8 (over y, x, core), tensor: 4 (over z).
Axes of the slice: x: 2, y: 2, z: 4, core: 2. Of those that a mesh axis runs over, the one named last changes fastest.
Arguments:
- activations: bfloat16 [4096, 4096], P('dp'), may hold values from -1000 to 1000
- norm_gain: bfloat16 [4096], replicated, may hold values from 0.5 to 1.5
- query_blocks: bfloat16 [128, 32, 4096], P('dp', None, 'tensor'), may hold values from -64 to 64
- query_scales: int32 [128, 1, 4096], P('dp', None, 'tensor'), may hold values from -9 to -5
- key_blocks: bfloat16 [128, 32, 512], P('dp', None, 'tensor'), may hold values from -64 to 64
- key_scales: int32 [128, 1, 512], P('dp', None, 'tensor'), may hold values from -9 to -5
- value_blocks: bfloat16 [128, 32, 512], P('dp', None, 'tensor'), may hold values from -6 to 6
- value_scales: int32 [128, 1, 512], P('dp', None, 'tensor'), may hold values from -9 to -5
- output_blocks: bfloat16 [128, 32, 4096], P('tensor', None, 'dp'), may hold values from -6 to 6
- output_scales: int32 [128, 1, 4096], P('tensor', None, 'dp'), may hold values from -9 to -5
Outputs:
- attended: bfloat16 [4096, 4096], P('dp')
All inputs are finite; a program needn't handle non-finite values.
Results may differ from a plain program's by a relative error of at most 0.015.
The roundings to bfloat16 on the way count: a program that leaves them out, or rounds other values in their place, can miss the bound.
Values may be sent and summed in bfloat16 or wider, within the bound.
No kernel may reach another device: no remote copies, remote signals or barrier semaphores. Data moves between devices by JAX's collectives and lax.ppermute only.
A program may use at most 128 MiB of HBM per device.

v0:
```python
import math
import jax
import jax.numpy as jnp
from jax import lax
from jax.sharding import PartitionSpec as P

HEAD_DIM = 128
SEQ = 256
EPS = 1e-05
ROPE_BASE = 500000.0


def dequant(blocks, scales):
    factor = jnp.exp2(scales.astype(jnp.float32)).astype(blocks.dtype)
    weight = blocks * factor
    return weight.reshape(weight.shape[0] * weight.shape[1], weight.shape[2])


def rotate_pairs(states, positions):
    half_dim = states.shape[-1] // 2
    frequency = jnp.exp(
        -math.log(ROPE_BASE) * jnp.arange(half_dim, dtype=jnp.float32) * 2.0 / states.shape[-1]
    )
    angles = positions.astype(jnp.float32)[:, None] * frequency[None, :]
    cosine = jnp.cos(angles)[None, :, None, :]
    sine_part = jnp.sin(angles)[None, :, None, :]
    first = states[..., :half_dim]
    second = states[..., half_dim:]
    return jnp.concatenate(
        [first * cosine - second * sine_part, second * cosine + first * sine_part], axis=-1
    )


def attend(query_states, key_states, value_states, kv_count):
    tokens_here = query_states.shape[0]
    count = tokens_here // SEQ
    positions = jnp.arange(SEQ, dtype=jnp.int32)
    queries = rotate_pairs(query_states.reshape(count, SEQ, -1, HEAD_DIM), positions).astype(
        jnp.bfloat16
    )
    rotated_keys = rotate_pairs(
        key_states.reshape(count, SEQ, kv_count, HEAD_DIM), positions
    ).astype(jnp.bfloat16)
    value_heads = value_states.astype(jnp.bfloat16).reshape(count, SEQ, kv_count, HEAD_DIM)
    group_size = queries.shape[2] // kv_count
    queries = queries.reshape(count, SEQ, kv_count, group_size, HEAD_DIM)
    scores = jnp.einsum(
        "sqkgd,stkd->skgqt", queries, rotated_keys, preferred_element_type=jnp.float32
    ) * HEAD_DIM ** (-0.5)
    visible = positions[:, None] >= positions[None, :]
    scores = jnp.where(visible, scores, -jnp.inf)
    attn_weights = jax.nn.softmax(scores, axis=-1).astype(jnp.bfloat16)
    context = jnp.einsum(
        "skgqt,stkd->sqkgd", attn_weights, value_heads, preferred_element_type=jnp.float32
    )
    return context.astype(jnp.bfloat16).reshape(tokens_here, -1)


def shards(
    activations,
    norm_gain,
    query_blocks,
    query_scales,
    key_blocks,
    key_scales,
    value_blocks,
    value_scales,
    output_blocks,
    output_scales,
):
    query_exps = query_scales.astype(jnp.bfloat16)
    key_exps = key_scales.astype(jnp.bfloat16)
    value_exps = value_scales.astype(jnp.bfloat16)
    output_exps = output_scales.astype(jnp.bfloat16)
    wide_rows = activations.astype(jnp.float32)
    inverse = lax.rsqrt(jnp.mean(wide_rows * wide_rows, axis=-1, keepdims=True) + EPS)
    normed = (wide_rows * inverse * norm_gain.astype(jnp.float32)).astype(jnp.bfloat16)

    def product(blocks, scales):
        return jnp.dot(normed, dequant(blocks, scales), preferred_element_type=jnp.float32)

    def add_one(pieces):
        return product(pieces[0], pieces[1])

    query_states = add_one(
        (
            lax.all_gather(query_blocks, "dp", axis=0, tiled=True),
            lax.all_gather(query_exps, "dp", axis=0, tiled=True),
        )
    )
    key_states = add_one(
        (
            lax.all_gather(key_blocks, "dp", axis=0, tiled=True),
            lax.all_gather(key_exps, "dp", axis=0, tiled=True),
        )
    )
    value_states = add_one(
        (
            lax.all_gather(value_blocks, "dp", axis=0, tiled=True),
            lax.all_gather(value_exps, "dp", axis=0, tiled=True),
        )
    )
    context = attend(query_states, key_states, value_states, key_blocks.shape[2] // HEAD_DIM)
    pieces = (
        lax.all_gather(output_blocks, "dp", axis=2, tiled=True),
        lax.all_gather(output_exps, "dp", axis=2, tiled=True),
    )
    block_out = jnp.dot(context, dequant(pieces[0], pieces[1]), preferred_element_type=jnp.float32)
    return lax.psum(block_out.astype(jnp.bfloat16), "tensor")


def solution(mesh):
    placed = (
        P("dp", None),
        P(),
        P("dp", None, "tensor"),
        P("dp", None, "tensor"),
        P("dp", None, "tensor"),
        P("dp", None, "tensor"),
        P("dp", None, "tensor"),
        P("dp", None, "tensor"),
        P("tensor", None, "dp"),
        P("tensor", None, "dp"),
    )
    return jax.shard_map(
        shards, mesh=mesh, in_specs=placed, out_specs=P("dp", None), check_vma=False
    )
```

profile of v0, /device:TPU:0, one launch (start us, length us, event | category | flops | bytes accessed | tf_op | source)
XLA Modules:
  0.0 358.5 jit_solution(17838992438456256269)
XLA Ops:
  6.5 0.7 all-gather.7.cloned.1.call-update
  7.3 0.7 all-gather.5.cloned.1.call-update
  8.1 0.7 all-gather.9.cloned.1.call-update
  8.8 0.5 all-gather.11.cloned.1.call-update
  9.4 0.9 convert_element_type.93
  10.2 0.9 convert_element_type.99
  11.1 0.7 convert_element_type.95
  11.8 0.9 convert_element_type.110
  12.7 12.4 %all_gather.31 = bf16[32,1,4096]{2,1,0:T(2,128)(2,1)S(1)} all-gather(bf16[32,1,512]{2,1,0:T(2,128)(2,1)S(1)} %convert_element_type.110), channel_id=1, replica_groups=mesh['dp'=8,'tensor'=4] {'dp'}, dimensions={2}, use_global_device_ids=true | all-gather | bytes 294912 | tf_op jit(solution)/shard_map/all_gather | solution.py:106
  25.1 0.9 exponential_convert_fusion
  26.4 9.1 %all_gather.27 = bf16[128,1,128]{2,0,1:T(8,128)(2,1)S(1)} all-gather(bf16[16,1,128]{2,0,1:T(8,128)(2,1)S(1)} %convert_element_type.99), channel_id=1, replica_groups=mesh['dp'=8,'tensor'=4] {'dp'}, dimensions={0}, use_global_device_ids=true | all-gather | bytes 36864 | tf_op jit(solution)/shard_map/all_gather | solution.py:94
  35.5 8.3 %all_gather.25 = bf16[128,1,128]{2,0,1:T(8,128)(2,1)S(1)} all-gather(bf16[16,1,128]{2,0,1:T(8,128)(2,1)S(1)} %convert_element_type.95), channel_id=1, replica_groups=mesh['dp'=8,'tensor'=4] {'dp'}, dimensions={0}, use_global_device_ids=true | all-gather | bytes 36864 | tf_op jit(solution)/shard_map/all_gather | solution.py:100
  43.8 9.4 %all_gather.29 = bf16[128,1,1024]{2,0,1:T(8,128)(2,1)S(1)} all-gather(bf16[16,1,1024]{2,0,1:T(8,128)(2,1)S(1)} %copy_convert_fusion), channel_id=1, replica_groups=mesh['dp'=8,'tensor'=4] {'dp'}, dimensions={0}, use_global_device_ids=true | all-gather | bytes 294912 | tf_op jit(solution)/shard_map/all_gather | solution.py:88
  53.2 3.1 fusion
  56.8 3.6 %fusion.2 = bf16[512,4096]{1,0:T(8,128)(2,1)} fusion(bf16[512,4096]{1,0:T(8,128)(2,1)S(1)} %copy-done, f32[4096]{0:T(1024)S(1)} %convert_element_type.93, f32[512]{0:T(512)S(1)} %add_rsqrt_fusion), kind=kLoop, calls=%fused_computation.4 | loop fusion | flops 8388608 | bytes 8407040 | tf_op jit(solution)/shard_map/convert_element_type | solution.py:77
  60.4 1.3 broadcast_multiply_fusion.2
  61.8 3.7 %convolution_bitcast_fusion = f32[2,256,1,128]{1,3,0,2:T(8,128)S(1)} fusion(bf16[2,256,4096]{2,1,0:T(8,128)(2,1)} %bitcast.88, bf16[4096,128,1]{1,0,2:T(8,128)(2,1)S(1)} %bitcast.92), kind=kOutput, calls=%fused_computation.18 | convolution fusion | flops 536870912 | bytes 5505024 | tf_op jit(solution)/shard_map/dot_general | solution.py:80
  65.5 1.3 broadcast_multiply_fusion.3
  66.8 3.4 convolution_convert_fusion.1
  70.3 47.6 %all-gather.9.cloned.1.call-done = bf16[128,32,1024]{2,1,0:T(8,128)(2,1)} async-done(((bf16[16,32,1024]{2,1,0:T(8,128)(2,1)}), bf16[128,32,1024]{2,1,0:T(8,128)(2,1)}) %all-gather.9.cloned.1.call-update) | async-done | bytes 8388624 | tf_op jit(solution)/shard_map/all_gather | solution.py:87
  117.9 7.2 %broadcast_multiply_fusion.1 = bf16[128,32,1024]{2,1,0:T(8,128)(2,1)} fusion(bf16[128,32,1024]{2,1,0:T(8,128)(2,1)} %all-gather.9.cloned.1.call-done, bf16[128,1024]{1,0:T(8,128)(2,1)S(1)} %fusion.20), kind=kLoop, calls=%fused_computation.10 | loop fusion | flops 4194304 | bytes 17039360 | tf_op jit(solution)/shard_map/mul | solution.py:15
  125.1 12.1 %copy.28 = bf16[1024,4096]{1,0:T(8,128)(2,1)} copy(bf16[1024,4096]{0,1:T(8,128)(2,1)} %bitcast.87) | data formatting | bytes 16777216 | tf_op jit(solution)/shard_map/dot_general | solution.py:80
  137.2 8.2 %fusion.30 = f32[2,256,8,128]{1,3,2,0:T(8,128)S(1)} fusion(bf16[2,256,4096,1]{2,1,3,0:T(8,128)(2,1)} %bitcast.89, bf16[8,128,4096,1]{2,1,0,3:T(8,128)(2,1)} %bitcast.91), kind=kOutput, calls=%fused_computation.55 | convolution fusion | flops 4294967296 | bytes 14680064 | tf_op jit(solution)/shard_map/dot_general | solution.py:80
  145.8 0.8 fusion.4
  146.6 0.9 fusion.3
  147.5 1.3 fusion.11
  148.8 0.8 copy.33
  149.5 26.0 %all-gather.11.cloned.1.call-done = bf16[32,32,4096]{2,1,0:T(8,128)(2,1)} async-done(((bf16[32,32,512]{2,1,0:T(8,128)(2,1)}), bf16[32,32,4096]{2,1,0:T(8,128)(2,1)}) %all-gather.11.cloned.1.call-update) | async-done | bytes 8388624 | tf_op jit(solution)/shard_map/all_gather | solution.py:105
  175.5 7.3 %broadcast_multiply_fusion = bf16[32,32,4096]{2,1,0:T(8,128)(2,1)} fusion(bf16[32,32,4096]{2,1,0:T(8,128)(2,1)} %all-gather.11.cloned.1.call-done, bf16[32,4096]{1,0:T(8,128)(2,1)S(1)} %bitcast.93), kind=kLoop, calls=%fused_computation.7 | loop fusion | flops 4194304 | bytes 17039360 | tf_op jit(solution)/shard_map/mul | solution.py:15
  182.8 9.4 %convolution_convert_fusion = bf16[512,4096]{1,0:T(8,128)(2,1)} fusion(bf16[1024,4096]{1,0:T(8,128)(2,1)} %bitcast.90, bf16[64,8,8,128]{3,2,1,0:T(8,128)(2,1)S(1)} %bitcast.94), kind=kOutput, calls=%fused_computation.5 | convolution fusion | flops 4297064448 | bytes 13631488 | tf_op jit(solution)/shard_map/dot_general | solution.py:108
  192.2 155.1 %all-reduce.2.cloned.1.call-done = bf16[512,4096]{1,0:T(8,128)(2,1)} async-done(((bf16[512,4096]{1,0:T(8,128)(2,1)}), bf16[512,4096]{1,0:T(8,128)(2,1)}) %all-reduce.2.cloned.1.call-update) | async-done | bytes 4194320 | tf_op jit(solution)/shard_map/psum | solution.py:109
  347.3 4.7 %copy.55 = bf16[512,4096]{1,0:T(8,128)(2,1)} copy(bf16[512,4096]{1,0:T(8,128)(2,1)} %all-reduce.2.cloned.1.call-done) | data formatting | bytes 8388608
  (24 shorter events, 1.4 us)
Async XLA Ops:
  6.5 37.2 %copy-start.1 = (s32[16,1,1024]{2,1,0:T(1,128)S(1)}, s32[16,1,1024]{2,1,0:T(1,128)}, u32[]{:S(2)}) copy-start(s32[16,1,1024]{2,1,0:T(1,128)} %param.13) | copy-start | bytes 196612
  6.5 53.9 %all-gather.7.cloned.1.call-start = ((), (), s32[]{:S(2)}) async-start(), calls=%async_computation.1 | async-start | bytes 1179648 | tf_op jit(solution)/shard_map/all_gather | solution.py:93
  7.3 58.3 %all-gather.5.cloned.1.call-start = ((), (), s32[]{:S(2)}) async-start(), calls=%async_computation | async-start | bytes 1179648 | tf_op jit(solution)/shard_map/all_gather | solution.py:99
  8.0 109.9 %all-gather.9.cloned.1.call-start = ((), (), s32[]{:S(2)}) async-start(), calls=%async_computation.2 | async-start | bytes 9437184 | tf_op jit(solution)/shard_map/all_gather | solution.py:87
  8.7 166.8 %all-gather.11.cloned.1.call-start = ((), (), s32[]{:S(2)}) async-start(), calls=%async_computation.3 | async-start | bytes 9437184 | tf_op jit(solution)/shard_map/all_gather | solution.py:105
  9.3 338.0 %all-reduce.2.cloned.1.call-start = ((), (), s32[]{:S(2)}) async-start(), calls=%async_computation.4 | async-start | bytes 8388608 | tf_op jit(solution)/shard_map/psum | solution.py:109
  9.4 47.4 %copy-start = (bf16[512,4096]{1,0:T(8,128)(2,1)S(1)}, bf16[512,4096]{1,0:T(8,128)(2,1)}, u32[]{:S(2)}) copy-start(bf16[512,4096]{1,0:T(8,128)(2,1)} %param.10) | copy-start | bytes 12582916
Sparse Core Ops, SparseCore 0:
  9.2 26.8 all-gather.6
  38.0 23.6 all-gather.4
  63.6 54.2 all-gather.8
  119.6 55.8 all-gather.10
  192.3 154.9 all-reduce.1
where the time goes:
time: 359 us
  waiting for transfers between devices  231 us (64%)
  blocking collectives  39.2 us (11%)
  other arithmetic  29.8 us (8%)
  matrix products  26.9 us (7%)
  local copies, waits for them, and re-layouts  17.9 us (5%)
  between operations  13.3 us (4%)
    psum x1, waiting for transfers between devices, shards(): return lax.psum(block_out.astype(jnp.bfloat16), 'tensor')  155 us
    all_gather x1, waiting for transfers between devices, shards(): lax.all_gather(query_blocks, 'dp', axis=0, tiled=True)  47.6 us
    all_gather x1, waiting for transfers between devices, shards(): lax.all_gather(output_blocks, 'dp', axis=2, tiled=True)  26 us
    mul x7, other arithmetic, dequant(): weight = blocks * factor  17.3 us
    dot_general x3, matrix products, product(): jnp.dot(normed, dequant(blocks, scales), preferred_element_type=jnp.float32)  15.4 us
    all_gather x1, blocking collectives, shards(): lax.all_gather(output_exps, 'dp', axis=2, tiled=True)  12.4 us
    dot_general x1, local copies, waits for them, and re-layouts, product(): jnp.dot(normed, dequant(blocks, scales), preferred_element_type=jnp.float32)  12.1 us
    all_gather x1, blocking collectives, shards(): lax.all_gather(query_exps, 'dp', axis=0, tiled=True)  9.4 us
  transfers between devices with their start and end apart: 5, of which 3 were waited for; matrix products, arithmetic and copies ran while one was open for 15% of the time, Pallas kernels for 0%

commit v1 on v0

--- a/solution.py
+++ b/solution.py
@@ -102,7 +102,7 @@
     )
     context = attend(query_states, key_states, value_states, key_blocks.shape[2] // HEAD_DIM)
     pieces = (
-        lax.all_gather(output_blocks, "dp", axis=2, tiled=True),
+        jnp.concatenate(lax.all_gather(output_blocks, "dp"), axis=2),
         lax.all_gather(output_exps, "dp", axis=2, tiled=True),
     )
     block_out = jnp.dot(context, dequant(pieces[0], pieces[1]), preferred_element_type=jnp.float32)

time: 359 us -> 374 us (1.042)
  local copies, waits for them, and re-layouts: 17.9 us -> 29.7 us
  other arithmetic: 29.8 us -> 34.8 us
    unnamed x6 -> x7, local copies, waits for them, and re-layouts: 5 us -> 17 us
    mul x7, other arithmetic: 17.3 us -> 21.2 us  [dequant(): weight = blocks * factor]
  transfers between devices with their start and end apart: 5 -> 5, of which waited for: 3 -> 3; matrix products, arithmetic and copies ran while one was open for 15% -> 14% of each run, Pallas kernels for 0% -> 0%
where the time goes in v1:
time: 374 us; the launch traced here: 373 us
  waiting for transfers between devices  229 us (61%)
  blocking collectives  39.2 us (10%)
  other arithmetic  34.8 us (9%)
  local copies, waits for them, and re-layouts  29.7 us (8%)
  matrix products  26.9 us (7%)
  between operations  13.3 us (4%)
    psum x1, waiting for transfers between devices, shards(): return lax.psum(block_out.astype(jnp.bfloat16), 'tensor')  155 us
    all_gather x1, waiting for transfers between devices, shards(): lax.all_gather(query_blocks, 'dp', axis=0, tiled=True)  46.9 us
    all_gather x1, waiting for transfers between devices, shards(): lax.all_gather(output_blocks, 'dp')  24.5 us
    mul x7, other arithmetic, dequant(): weight = blocks * factor  21.2 us
    unnamed x7, local copies, waits for them, and re-layouts  17 us
    dot_general x3, matrix products, product(): jnp.dot(normed, dequant(blocks, scales), preferred_element_type=jnp.float32)  15.4 us
    all_gather x1, blocking collectives, shards(): lax.all_gather(output_exps, 'dp', axis=2, tiled=True)  12.4 us
    dot_general x1, local copies, waits for them, and re-layouts, product(): jnp.dot(normed, dequant(blocks, scales), preferred_element_type=jnp.float32)  12 us
  transfers between devices with their start and end apart: 5, of which 3 were waited for; matrix products, arithmetic and copies ran while one was open for 14% of the time, Pallas kernels for 0%

profile of v1, /device:TPU:0, one launch (start us, length us, event | category | flops | bytes accessed | tf_op | source)
XLA Modules:
  0.0 373.2 jit_solution(4274897284583856472)
XLA Ops:
  6.5 0.7 all-gather.8.cloned.1.call-update
  7.3 0.7 all-gather.6.cloned.1.call-update
  8.1 0.7 all-gather.10.cloned.1.call-update
  9.4 0.9 convert_element_type.93
  10.2 0.9 convert_element_type.99
  11.1 0.7 convert_element_type.95
  11.8 0.9 convert_element_type.110
  12.7 12.4 %all_gather.35 = bf16[32,1,4096]{2,1,0:T(2,128)(2,1)S(1)} all-gather(bf16[32,1,512]{2,1,0:T(2,128)(2,1)S(1)} %convert_element_type.110), channel_id=1, replica_groups=mesh['dp'=8,'tensor'=4] {'dp'}, dimensions={2}, use_global_device_ids=true | all-gather | bytes 294912 | tf_op jit(solution)/shard_map/all_gather | solution.py:106
  25.1 1.8 convert_reduce_fusion
  27.0 9.1 %all_gather.30 = bf16[128,1,128]{2,0,1:T(8,128)(2,1)S(1)} all-gather(bf16[16,1,128]{2,0,1:T(8,128)(2,1)S(1)} %convert_element_type.99), channel_id=1, replica_groups=mesh['dp'=8,'tensor'=4] {'dp'}, dimensions={0}, use_global_device_ids=true | all-gather | bytes 36864 | tf_op jit(solution)/shard_map/all_gather | solution.py:94
  36.1 8.2 %all_gather.28 = bf16[128,1,128]{2,0,1:T(8,128)(2,1)S(1)} all-gather(bf16[16,1,128]{2,0,1:T(8,128)(2,1)S(1)} %convert_element_type.95), channel_id=1, replica_groups=mesh['dp'=8,'tensor'=4] {'dp'}, dimensions={0}, use_global_device_ids=true | all-gather | bytes 36864 | tf_op jit(solution)/shard_map/all_gather | solution.py:100
  44.4 9.4 %all_gather.32 = bf16[128,1,1024]{2,0,1:T(8,128)(2,1)S(1)} all-gather(bf16[16,1,1024]{2,0,1:T(8,128)(2,1)S(1)} %copy_convert_fusion), channel_id=1, replica_groups=mesh['dp'=8,'tensor'=4] {'dp'}, dimensions={0}, use_global_device_ids=true | all-gather | bytes 294912 | tf_op jit(solution)/shard_map/all_gather | solution.py:88
  53.8 3.3 fusion
  57.6 3.6 fusion.2
  61.2 1.3 broadcast_multiply_fusion.1
  62.5 3.7 convolution_bitcast_fusion
  66.3 1.3 broadcast_multiply_fusion.2
  67.6 3.4 convolution_convert_fusion.1
  71.1 46.9 %all-gather.10.cloned.1.call-done = bf16[128,32,1024]{2,1,0:T(8,128)(2,1)} async-done(((bf16[16,32,1024]{2,1,0:T(8,128)(2,1)}), bf16[128,32,1024]{2,1,0:T(8,128)(2,1)}) %all-gather.10.cloned.1.call-update) | async-done | bytes 8388624 | tf_op jit(solution)/shard_map/all_gather | solution.py:87
  117.9 7.2 %broadcast_multiply_fusion = bf16[128,32,1024]{2,1,0:T(8,128)(2,1)} fusion(bf16[128,32,1024]{2,1,0:T(8,128)(2,1)} %all-gather.10.cloned.1.call-done, bf16[128,1024]{1,0:T(8,128)(2,1)S(1)} %fusion.20), kind=kLoop, calls=%fused_computation.10 | loop fusion | flops 4194304 | bytes 17039360 | tf_op jit(solution)/shard_map/mul | solution.py:15
  125.2 12.0 %copy.30 = bf16[1024,4096]{1,0:T(8,128)(2,1)} copy(bf16[1024,4096]{0,1:T(8,128)(2,1)} %bitcast.91) | data formatting | bytes 16777216 | tf_op jit(solution)/shard_map/dot_general | solution.py:80
  137.1 8.2 %fusion.30 = f32[2,256,8,128]{1,3,2,0:T(8,128)S(1)} fusion(bf16[2,256,4096,1]{2,1,3,0:T(8,128)(2,1)} %bitcast.94, bf16[8,128,4096,1]{2,1,0,3:T(8,128)(2,1)} %bitcast.96), kind=kOutput, calls=%fused_computation.54 | convolution fusion | flops 4294967296 | bytes 14680064 | tf_op jit(solution)/shard_map/dot_general | solution.py:80
  145.7 0.8 fusion.4
  146.5 0.9 fusion.3
  147.4 1.3 fusion.11
  148.7 0.8 copy.35
  149.5 24.5 %all-gather.12.cloned.1.call-done = bf16[256,32,512]{2,1,0:T(8,128)(2,1)} async-done(((bf16[32,32,512]{2,1,0:T(8,128)(2,1)}), bf16[256,32,512]{2,1,0:T(8,128)(2,1)}) %all-gather.12.cloned.1.call-update) | async-done | bytes 8388624 | tf_op jit(solution)/shard_map/all_gather | solution.py:105
  174.0 11.2 %bitcast_multiply_fusion = bf16[32,32,8,512]{3,2,1,0:T(8,128)(2,1)} fusion(bf16[8,32,32,512]{3,2,1,0:T(8,128)(2,1)} %bitcast.95, bf16[32,8,512]{2,1,0:T(8,128)(2,1)S(1)} %bitcast.99), kind=kLoop, calls=%fused_computation.5 | loop fusion | flops 4194304 | bytes 17039360 | tf_op jit(solution)/shard_map/mul | solution.py:15
  185.2 12.2 %copy.50 = bf16[128,8,8,512]{3,1,2,0:T(8,128)(2,1)} copy(bf16[128,8,8,512]{3,2,1,0:T(8,128)(2,1)} %bitcast.92) | data formatting | bytes 16777216
  197.4 9.4 %convolution_convert_fusion = bf16[512,4096]{1,0:T(8,128)(2,1)} fusion(bf16[1024,4096]{1,0:T(8,128)(2,1)} %bitcast.97, bf16[64,8,8,128]{3,2,1,0:T(8,128)(2,1)S(1)} %bitcast.101), kind=kOutput, calls=%fused_computation.6 | convolution fusion | flops 4297064448 | bytes 13631488 | tf_op jit(solution)/shard_map/dot_general | solution.py:108
  206.8 155.1 %all-reduce.2.cloned.1.call-done = bf16[512,4096]{1,0:T(8,128)(2,1)} async-done(((bf16[512,4096]{1,0:T(8,128)(2,1)}), bf16[512,4096]{1,0:T(8,128)(2,1)}) %all-reduce.2.cloned.1.call-update) | async-done | bytes 4194320 | tf_op jit(solution)/shard_map/psum | solution.py:109
  361.9 4.7 %copy.58 = bf16[512,4096]{1,0:T(8,128)(2,1)} copy(bf16[512,4096]{1,0:T(8,128)(2,1)} %all-reduce.2.cloned.1.call-done) | data formatting | bytes 8388608
  (25 shorter events, 1.7 us)
Async XLA Ops:
  6.5 37.8 %copy-start.1 = (s32[16,1,1024]{2,1,0:T(1,128)S(1)}, s32[16,1,1024]{2,1,0:T(1,128)}, u32[]{:S(2)}) copy-start(s32[16,1,1024]{2,1,0:T(1,128)} %param.13) | copy-start | bytes 196612
  6.5 54.7 %all-gather.8.cloned.1.call-start = ((), (), s32[]{:S(2)}) async-start(), calls=%async_computation.1 | async-start | bytes 1179648 | tf_op jit(solution)/shard_map/all_gather | solution.py:93
  7.3 59.0 %all-gather.6.cloned.1.call-start = ((), (), s32[]{:S(2)}) async-start(), calls=%async_computation | async-start | bytes 1179648 | tf_op jit(solution)/shard_map/all_gather | solution.py:99
  8.0 109.9 %all-gather.10.cloned.1.call-start = ((), (), s32[]{:S(2)}) async-start(), calls=%async_computation.2 | async-start | bytes 9437184 | tf_op jit(solution)/shard_map/all_gather | solution.py:87
  8.7 165.2 %all-gather.12.cloned.1.call-start = ((), (), s32[]{:S(2)}) async-start(), calls=%async_computation.4 | async-start | bytes 9437184 | tf_op jit(solution)/shard_map/all_gather | solution.py:105
  9.3 352.6 %all-reduce.2.cloned.1.call-start = ((), (), s32[]{:S(2)}) async-start(), calls=%async_computation.3 | async-start | bytes 8388608 | tf_op jit(solution)/shard_map/psum | solution.py:109
  9.4 48.2 %copy-start = (bf16[512,4096]{1,0:T(8,128)(2,1)S(1)}, bf16[512,4096]{1,0:T(8,128)(2,1)}, u32[]{:S(2)}) copy-start(bf16[512,4096]{1,0:T(8,128)(2,1)} %param.10) | copy-start | bytes 12582916
Sparse Core Ops, SparseCore 0:
  9.2 26.7 all-gather.7
  37.9 23.8 all-gather.5
  63.6 54.2 all-gather.9
  119.7 54.2 all-gather.11
  206.9 154.9 all-reduce.1
